TPU v7x, 256 devices: a whole 4x4x8 slice. The times are simulated.
256 devices in a mesh: blk: 32 (over x_hi, z, core), req: 8 (over y, x_lo).
Axes of the slice: x: 4 (x_hi: 2, x_lo: 2; x = x_hi * 2 + x_lo), y: 4, z: 8, core: 2. Of those that a mesh axis runs over, the one named last changes fastest.
Arguments:
- prefill_queries: bfloat16 [8, 512, 1024], P('req', 'blk'), may hold values from -6 to 6
- decode_queries: bfloat16 [128, 1024], P('req'), may hold values from -6 to 6
- new_prefill: bfloat16 [8, 512, 512], P('req', 'blk'), may hold values from -6 to 6
- new_decode: bfloat16 [128, 512], P('req'), may hold values from -6 to 6
- prefill_cache: bfloat16 [8, 4096, 512], P('req', 'blk'), may hold values from -5 to 5
- decode_cache: bfloat16 [128, 4096, 512], P('req', 'blk'), may hold values from -5 to 5
- prefill_offsets: int32 [8], P('req'), may hold values from 2 to 3584, as said below
- decode_lengths: int32 [128], P('req'), may hold values from 2 to 4095, as said below
- dealing: int32 [136], replicated, may hold values from 0 to 127, as said below
Outputs:
- prefill_out: bfloat16 [8, 512, 1024], P('req', 'blk')
- decode_out: bfloat16 [128, 1024], P('req')
- prefill_cache_out: bfloat16 [8, 4096, 512], P('req', 'blk')
- decode_cache_out: bfloat16 [128, 4096, 512], P('req', 'blk')
Inputs may be any that keep to these rules, and one draw needn't show every extreme that they name: The block of prefill slot i fills positions prefill_offsets[i] to prefill_offsets[i] + 511; some slot has offset 4096 - 512. The new token of decode slot j goes to position decode_lengths[j]; some slot has length 4095. `dealing`: the first 8 entries are a permutation of 0 to 7, the other 128 a permutation of 0 to 127.
All inputs are finite; a program needn't handle non-finite values.
Results may differ from a plain program's by a relative error of at most 0.0085.
Values may be sent and summed in bfloat16 or wider, within the bound.
A program may use at most 64 MiB of HBM per device.

v0:
```python
import jax
import jax.numpy as jnp
from jax import lax
from jax.sharding import PartitionSpec as P

QUERY_HEADS = 8
KEY_VALUE_HEADS = 2
HEAD_SIZE = 128
masked_fill = -1e30


def merged(part, axis, combine):
    gathered = jax.tree.map(lambda a: lax.all_gather(a, axis), part)

    def take(source):
        return jax.tree.map(lambda a: lax.dynamic_index_in_dim(a, source, 0, False), gathered)

    return lax.fori_loop(
        1, lax.axis_size(axis), lambda source, state: combine(state, take(source)), take(0)
    )


def write_block(cache_table, block_rows, offsets, positions):
    piece_len = block_rows.shape[1]
    relative = positions[None, :] - offsets[:, None]
    picked = jax.vmap(lambda source_rows, row_index: source_rows[row_index])(
        block_rows, jnp.clip(relative, 0, piece_len - 1)
    )
    inside = (relative >= 0) & (relative < piece_len)
    return jnp.where(inside[:, :, None], picked, cache_table)


def scores_of(query_rows, cache_table, limits, key_pos):
    slot_total, row_total = (query_rows.shape[0], query_rows.shape[1])
    column_total = cache_table.shape[1]
    grouped_queries = query_rows.reshape(
        slot_total, row_total, KEY_VALUE_HEADS, QUERY_HEADS // KEY_VALUE_HEADS, HEAD_SIZE
    )
    key_portion = cache_table[:, :, : KEY_VALUE_HEADS * HEAD_SIZE].reshape(
        slot_total, column_total, KEY_VALUE_HEADS, HEAD_SIZE
    )
    scores = jnp.einsum(
        "nrgqd,ncgd->ngqrc", grouped_queries, key_portion, preferred_element_type=jnp.float32
    ) * HEAD_SIZE ** (-0.5)
    visible = (key_pos[None, None, :] <= limits[:, :, None])[:, None, None]
    return (jnp.where(visible, scores, masked_fill), visible)


def weigh_values(scores, visible, maxima, cache_table):
    slot_total, column_total = (cache_table.shape[0], cache_table.shape[1])
    exponent = jnp.where(visible, jnp.exp(scores - maxima[..., None]), 0.0)
    value_portion = cache_table[:, :, KEY_VALUE_HEADS * HEAD_SIZE :].reshape(
        slot_total, column_total, KEY_VALUE_HEADS, HEAD_SIZE
    )
    weighted = jnp.einsum(
        "ngqrc,ncgd->ngqrd",
        exponent.astype(jnp.bfloat16),
        value_portion,
        preferred_element_type=jnp.float32,
    )
    return (jnp.sum(exponent, axis=-1), weighted)


def finish_rows(totals, weighted):
    normed = weighted / totals[..., None]
    slot_total, row_total = (normed.shape[0], normed.shape[3])
    return (
        jnp.transpose(normed, (0, 3, 1, 2, 4))
        .reshape(slot_total, row_total, QUERY_HEADS * HEAD_SIZE)
        .astype(jnp.bfloat16)
    )


def combine(first, second):
    first_max, first_total, first_sum = first
    second_max, second_total, second_sum = second
    joined = jnp.maximum(first_max, second_max)
    first_scale = jnp.exp(first_max - joined)
    second_scale = jnp.exp(second_max - joined)
    return (
        joined,
        first_total * first_scale + second_total * second_scale,
        first_sum * first_scale[..., None] + second_sum * second_scale[..., None],
    )


def per_device(
    prefill_queries,
    decode_queries,
    new_prefill,
    new_decode,
    prefill_cache,
    decode_cache,
    prefill_offsets,
    decode_lengths,
    dealing,
):
    ctx_dev = prefill_cache.shape[1]
    blk_index = lax.axis_index("blk")
    positions = blk_index * ctx_dev + jnp.arange(ctx_dev, dtype=jnp.int32)
    written = positions[None, :] == decode_lengths[:, None]
    decode_cache_out = jnp.where(written[:, :, None], new_decode[:, None, :], decode_cache)
    dec_scores, dec_visible = scores_of(
        decode_queries[:, None, :], decode_cache_out, decode_lengths[:, None], positions
    )
    dec_max = jnp.max(dec_scores, axis=-1)
    dec_total, dec_sum = weigh_values(dec_scores, dec_visible, dec_max, decode_cache_out)
    dec_max, dec_total, dec_sum = merged((dec_max, dec_total, dec_sum), "blk", combine)
    decode_attn = finish_rows(dec_total, dec_sum)[:, 0, :]
    block_rows, whole_queries = (
        lax.all_gather(new_prefill, "blk", axis=1, tiled=True),
        lax.all_gather(prefill_queries, "blk", axis=1, tiled=True),
    )
    prefill_cache_out = write_block(prefill_cache, block_rows, prefill_offsets, positions)
    limits = prefill_offsets[:, None] + jnp.arange(whole_queries.shape[1], dtype=jnp.int32)[None, :]
    scores, visible = scores_of(whole_queries, prefill_cache_out, limits, positions)
    maxima = jnp.max(scores, axis=-1)
    totals, weighted = weigh_values(scores, visible, maxima, prefill_cache_out)
    peer_max, peer_total, peer_sum = (
        lax.all_to_all(maxima[None], "blk", split_axis=4, concat_axis=0, tiled=True),
        lax.all_to_all(totals[None], "blk", split_axis=4, concat_axis=0, tiled=True),
        lax.all_to_all(weighted[None], "blk", split_axis=4, concat_axis=0, tiled=True),
    )
    joined = jnp.max(peer_max, axis=0)
    peer_scale = jnp.exp(peer_max - joined[None])
    totals = jnp.sum(peer_total * peer_scale, axis=0)
    weighted = jnp.sum(peer_sum * peer_scale[..., None], axis=0)
    prefill_attn = finish_rows(totals, weighted)
    gathered_pre, gathered_dec = (
        lax.all_gather(prefill_attn, "req", axis=0, tiled=True),
        lax.all_gather(decode_attn, "req", axis=0, tiled=True),
    )
    group_index = lax.axis_index("req")
    pre_count = prefill_attn.shape[0]
    dec_count = decode_attn.shape[0]
    total_pre = gathered_pre.shape[0]
    own_pre = group_index * pre_count + jnp.arange(pre_count, dtype=jnp.int32)
    own_dec = group_index * dec_count + jnp.arange(dec_count, dtype=jnp.int32)
    pre_selector = (dealing[:total_pre][None, :] == own_pre[:, None]).astype(jnp.bfloat16)
    dec_selector = (dealing[total_pre:][None, :] == own_dec[:, None]).astype(jnp.bfloat16)
    prefill_out = jnp.einsum(
        "rs,sbf->rbf", pre_selector, gathered_pre, preferred_element_type=jnp.float32
    ).astype(jnp.bfloat16)
    decode_out = jnp.dot(dec_selector, gathered_dec, preferred_element_type=jnp.float32).astype(
        jnp.bfloat16
    )
    return (prefill_out, decode_out, prefill_cache_out, decode_cache_out)


def solution(mesh):
    in_specs = (
        P("req", "blk", None),
        P("req", None),
        P("req", "blk", None),
        P("req", None),
        P("req", "blk", None),
        P("req", "blk", None),
        P("req"),
        P("req"),
        P(),
    )
    out_specs = (
        P("req", "blk", None),
        P("req", None),
        P("req", "blk", None),
        P("req", "blk", None),
    )
    return jax.shard_map(
        per_device, mesh=mesh, in_specs=in_specs, out_specs=out_specs, check_vma=False
    )
```

profile of v0, /device:TPU:6, one launch (start us, length us, event | category | flops | bytes accessed | tf_op | source)
XLA Modules:
  0.0 344.9 jit_solution(14435808164075506)
XLA Ops:
  8.0 3.9 %copy.83 = bf16[16,128,512]{1,2,0:T(8,128)(2,1)} copy(bf16[16,128,512]{2,1,0:T(8,128)(2,1)} %param.16) | data formatting | bytes 4194304 | tf_op args[5]
  12.0 2.5 broadcast_select_fusion
  15.1 1.3 fusion.28
  16.5 2.6 copy.95
  19.8 44.6 %all_gather.30 = bf16[1,512,512]{2,1,0:T(8,128)(2,1)S(1)} all-gather(bf16[1,16,512]{2,1,0:T(8,128)(2,1)S(1)} %copy-done.4), channel_id=1, replica_groups=mesh['blk'=32,'req'=8] {'blk'}, dimensions={1}, use_global_device_ids=true | all-gather | bytes 540672 | tf_op jit(solution)/shard_map/all_gather | solution.py:111
  64.4 1.2 gather_fusion
  65.9 38.4 %all-gather = f32[512,2,4]{2,1,0:T(2,128)S(1)} all-gather(f32[16,2,4]{2,1,0:T(2,128)S(1)} %get-tuple-element.249), channel_id=2, replica_groups=mesh['blk'=32,'req'=8] {'blk'}, dimensions={0}, use_global_device_ids=true | all-gather | bytes 16896 | tf_op jit(solution)/shard_map/all_gather | solution.py:13
  104.6 39.6 %all-gather.1 = f32[512,2,4]{2,1,0:T(2,128)S(1)} all-gather(f32[16,2,4]{2,1,0:T(2,128)S(1)} %fusion.26), channel_id=3, replica_groups=mesh['blk'=32,'req'=8] {'blk'}, dimensions={0}, use_global_device_ids=true | all-gather | bytes 16896 | tf_op jit(solution)/shard_map/all_gather | solution.py:13
  144.3 1.1 copy.91
  145.4 1.1 copy.92
  146.8 1.5 copy.70
  149.1 1.4 reshape.386
  150.5 5.5 %all-to-all-start.1 = ((f32[32,1,128]{2,1,0:T(1,128)}), f32[32,1,128]{2,1,0:T(1,128)S(1)}, u32[]{:S(2)}, u32[]{:S(2)}) async-start(f32[32,1,128]{2,1,0:T(1,128)} %reshape.386), calls=%async_computation.1 | async-start | bytes 32768 | tf_op jit(solution)/shard_map/all_to_all | solution.py:120
  156.8 1.4 reshape.388
  158.2 4.9 %all-to-all-done.1 = f32[32,1,128]{2,1,0:T(1,128)S(1)} async-done(((f32[32,1,128]{2,1,0:T(1,128)}), f32[32,1,128]{2,1,0:T(1,128)S(1)}, u32[]{:S(2)}, u32[]{:S(2)}) %all-to-all-start.1) | async-done | bytes 16416 | tf_op jit(solution)/shard_map/all_to_all | solution.py:120
  163.1 6.7 %all-to-all-start.2 = ((f32[32,1,128]{2,1,0:T(1,128)}), f32[32,1,128]{2,1,0:T(1,128)S(1)}, u32[]{:S(2)}, u32[]{:S(2)}) async-start(f32[32,1,128]{2,1,0:T(1,128)} %reshape.388), calls=%async_computation.2 | async-start | bytes 32768 | tf_op jit(solution)/shard_map/all_to_all | solution.py:121
  170.5 2.6 copy.76
  175.8 1.0 all-to-all-done.2
  176.8 8.8 %all-to-all-start = ((f32[1,1,2,4,512,128]{5,3,2,1,0,4:T(4,128)}), f32[1,1,2,4,512,128]{5,3,2,1,0,4:T(4,128)S(1)}, u32[]{:S(2)}, u32[]{:S(2)}) async-start(f32[1,1,2,4,512,128]{5,3,2,1,0,4:T(4,128)} %copy.76), calls=%async_computation | async-start | bytes 4194304 | tf_op jit(solution)/shard_map/all_to_all | solution.py:122
  188.7 88.2 %while.19 = (s32[]{:T(128)}, f32[16,2,4,1]{0,2,3,1:T(4,128)S(1)}, f32[16,2,4,1]{0,2,3,1:T(4,128)S(1)}, f32[16,2,4,1,128]{4,3,2,1,0:T(1,128)S(1)}, f32[32,16,2,4,...) while((s32[]{:T(128)}, f32[16,2,4,1]{0,2,3,1:T(4,128)S(1)}, ...), condition=%wide.region_8.9_spmd, body=%wide.region_7.8_spmd.sunk | while | flops 50053 | bytes 337563 | solution.py:18
  190.1 0.9 constant_dynamic-slice_fusion.2
  192.9 0.9 constant_dynamic-slice_fusion.2
  195.8 0.9 constant_dynamic-slice_fusion.2
  198.6 0.9 constant_dynamic-slice_fusion.2
  204.3 0.9 constant_dynamic-slice_fusion.2
  210.0 0.9 constant_dynamic-slice_fusion.2
  215.7 0.9 constant_dynamic-slice_fusion.2
  227.2 0.9 constant_dynamic-slice_fusion.2
  230.0 0.9 constant_dynamic-slice_fusion.2
  247.1 0.9 constant_dynamic-slice_fusion.2
  277.4 29.2 %all_gather.39 = bf16[128,1024]{1,0:T(8,128)(2,1)S(1)} all-gather(bf16[16,1024]{1,0:T(8,128)(2,1)S(1)} %convert_element_type.51), channel_id=1, replica_groups=mesh['blk'=32,'req'=8] {'req'}, dimensions={0}, use_global_device_ids=true | all-gather | bytes 294912 | tf_op jit(solution)/shard_map/all_gather | solution.py:131
  308.2 28.9 %all_gather.32 = bf16[8,16,1024]{2,1,0:T(8,128)(2,1)S(1)} all-gather(bf16[1,16,1024]{2,1,0:T(8,128)(2,1)S(1)} %convert_element_type.46), channel_id=1, replica_groups=mesh['blk'=32,'req'=8] {'req'}, dimensions={0}, use_global_device_ids=true | all-gather | bytes 294912 | tf_op jit(solution)/shard_map/all_gather | solution.py:130
  (276 shorter events, 92.5 us)
Async XLA Ops:
  7.2 139.6 %all-gather.6.cloned.1.call-start = ((), (), s32[]{:S(2)}) async-start(), calls=%async_computation.3 | async-start | bytes 1081344 | tf_op jit(solution)/shard_map/all_gather | solution.py:112
  7.9 179.9 %all-gather.8.cloned.1.call-start = ((), (), s32[]{:S(2)}) async-start(), calls=%async_computation.4 | async-start | bytes 2162688 | tf_op jit(solution)/shard_map/all_gather | solution.py:13
  8.0 4.0 %copy-start.2 = (bf16[16,1024]{1,0:T(8,128)(2,1)S(1)}, bf16[16,1024]{1,0:T(8,128)(2,1)}, u32[]{:S(2)}) copy-start(bf16[16,1024]{1,0:T(8,128)(2,1)} %param.12) | copy-start | bytes 98308
  8.0 4.0 %copy-start.6 = (s32[16]{0:T(128)S(1)}, s32[16]{0:T(128)}, u32[]{:S(2)}) copy-start(s32[16]{0:T(128)} %param.18) | copy-start | bytes 196
  8.0 4.1 %copy-start.3 = (bf16[16,512]{1,0:T(8,128)(2,1)S(1)}, bf16[16,512]{1,0:T(8,128)(2,1)}, u32[]{:S(2)}) copy-start(bf16[16,512]{1,0:T(8,128)(2,1)} %param.14) | copy-start | bytes 49156
  16.5 3.3 copy-start.4
  16.5 49.1 %copy-start.1 = (bf16[1,128,512]{2,1,0:T(8,128)(2,1)S(1)}, bf16[1,128,512]{2,1,0:T(8,128)(2,1)}, u32[]{:S(2)}) copy-start(bf16[1,128,512]{2,1,0:T(8,128)(2,1)} %param.15) | copy-start | bytes 393220
  64.4 82.2 %copy-start.5 = (s32[136]{0:T(256)S(1)}, s32[136]{0:T(256)}, u32[]{:S(2)}) copy-start(s32[136]{0:T(256)} %param.19) | copy-start | bytes 1636
  65.7 82.6 %copy-start = (bf16[1,128,512]{2,1,0:T(8,128)(2,1)}, bf16[1,128,512]{2,1,0:T(8,128)(2,1)S(1)}, u32[]{:S(2)}) copy-start(bf16[1,128,512]{2,1,0:T(8,128)(2,1)S(1)} %bitcast_select_fusion.1) | copy-start | bytes 393220
  150.5 12.6 %all-to-all-start.1 = ((f32[32,1,128]{2,1,0:T(1,128)}), f32[32,1,128]{2,1,0:T(1,128)S(1)}, u32[]{:S(2)}, u32[]{:S(2)}) async-start(f32[32,1,128]{2,1,0:T(1,128)} %reshape.386), calls=%async_computation.1 | async-start | bytes 32768 | tf_op jit(solution)/shard_map/all_to_all | solution.py:120
  163.1 13.7 %all-to-all-start.2 = ((f32[32,1,128]{2,1,0:T(1,128)}), f32[32,1,128]{2,1,0:T(1,128)S(1)}, u32[]{:S(2)}, u32[]{:S(2)}) async-start(f32[32,1,128]{2,1,0:T(1,128)} %reshape.388), calls=%async_computation.2 | async-start | bytes 32768 | tf_op jit(solution)/shard_map/all_to_all | solution.py:121
  176.8 130.6 %all-to-all-start = ((f32[1,1,2,4,512,128]{5,3,2,1,0,4:T(4,128)}), f32[1,1,2,4,512,128]{5,3,2,1,0,4:T(4,128)S(1)}, u32[]{:S(2)}, u32[]{:S(2)}) async-start(f32[1,1,2,4,512,128]{5,3,2,1,0,4:T(4,128)} %copy.76), calls=%async_computation | async-start | bytes 4194304 | tf_op jit(solution)/shard_map/all_to_all | solution.py:122
Sparse Core Ops, SparseCore 0:
  10.8 79.0 all-gather.5
  92.7 76.8 all-gather.7
where the time goes:
time: 349 us; the launch traced here: 345 us
  blocking collectives  181 us (52%)
  other arithmetic  61.4 us (18%)
  local copies, waits for them, and re-layouts  55.1 us (16%)
  starting transfers between devices  21.1 us (6%)
  between operations  15 us (4%)
  waiting for transfers between devices  6.66 us (2%)
  matrix products  4.23 us (1%)
    all_gather x2, blocking collectives, merged(): gathered = jax.tree.map(lambda a: lax.all_gather(a, axis), part)  77.9 us
    all_gather x1, blocking collectives, per_device(): lax.all_gather(new_prefill, 'blk', axis=1, tiled=True)  44.6 us
    all_gather x1, blocking collectives, per_device(): lax.all_gather(decode_attn, 'req', axis=0, tiled=True)  29.2 us
    all_gather x1, blocking collectives, per_device(): lax.all_gather(prefill_attn, 'req', axis=0, tiled=True)  28.9 us
    dynamic_slice x36, local copies, waits for them, and re-layouts, take(): lax.dynamic_index_in_dim(a, source, 0, False)  27.4 us
    mul x31, other arithmetic, combine(): second_sum * second_scale[..., None]  21.9 us
    mul x31, other arithmetic, combine(): first_sum * first_scale[..., None] + second_sum * second_scale[..., None]  21.4 us
    add x31, other arithmetic, combine(): first_sum * first_scale[..., None] + second_sum * second_scale[..., None]  12 us
  transfers between devices with their start and end apart: 5, of which 2 were waited for; matrix products, arithmetic and copies ran while one was open for 34% of the time, Pallas kernels for 0%

commit v1 on v0

--- a/solution.py
+++ b/solution.py
@@ -1,3 +1,4 @@
+import functools
 import jax
 import jax.numpy as jnp
 from jax import lax
@@ -7,6 +8,16 @@
 KEY_VALUE_HEADS = 2
 HEAD_SIZE = 128
 masked_fill = -1e30
+
+
+def _solve_rails(u_in, axis_name):
+    odd = lax.psum(1, axis_name)
+    ready = jnp.stack([u_in] * odd)
+    vec_out = lax.all_to_all(ready, axis_name, 0, 0)
+    return jnp.concatenate(vec_out, 1)
+
+
+_hold_zones = functools.partial(_solve_rails, axis_name="blk")
 
 
 def merged(part, axis, combine):
@@ -108,7 +119,7 @@
     dec_max, dec_total, dec_sum = merged((dec_max, dec_total, dec_sum), "blk", combine)
     decode_attn = finish_rows(dec_total, dec_sum)[:, 0, :]
     block_rows, whole_queries = (
-        lax.all_gather(new_prefill, "blk", axis=1, tiled=True),
+        _hold_zones(new_prefill),
         lax.all_gather(prefill_queries, "blk", axis=1, tiled=True),
     )
     prefill_cache_out = write_block(prefill_cache, block_rows, prefill_offsets, positions)

time: 349 us -> 337 us (0.966)
  blocking collectives: 181 us -> 140 us
  waiting for transfers between devices: 6.66 us -> 19.6 us
  starting transfers between devices: 21.1 us -> 33.3 us
    all_gather x1 -> x0, blocking collectives: 44.6 us -> none  [per_device(): lax.all_gather(new_prefill, 'blk', axis=1, tiled=True)]
    all_gather x1, waiting for transfers between devices: 0.02 us -> 13 us  [merged(): gathered = jax.tree.map(lambda a: lax.all_gather(a, axis), part)]
    all_to_all x0 -> x1, starting transfers between devices: none -> 11.6 us  [_solve_rails(): vec_out = lax.all_to_all(ready, axis_name, 0, 0)]
    all_gather x2, blocking collectives: 77.9 us -> 82.4 us  [merged(): gathered = jax.tree.map(lambda a: lax.all_gather(a, axis), part)]
  transfers between devices with their start and end apart: 5 -> 6, of which waited for: 2 -> 3; matrix products, arithmetic and copies ran while one was open for 34% -> 36% of each run, Pallas kernels for 0% -> 0%
where the time goes in v1:
time: 337 us; the launch traced here: 331 us
  blocking collectives  140 us (42%)
  other arithmetic  61.4 us (18%)
  local copies, waits for them, and re-layouts  56 us (17%)
  starting transfers between devices  33.3 us (10%)
  waiting for transfers between devices  19.6 us (6%)
  between operations  15.1 us (4%)
  matrix products  4.23 us (1%)
    all_gather x2, blocking collectives, merged(): gathered = jax.tree.map(lambda a: lax.all_gather(a, axis), part)  82.4 us
    all_gather x1, blocking collectives, per_device(): lax.all_gather(prefill_attn, 'req', axis=0, tiled=True)  29 us
    all_gather x1, blocking collectives, per_device(): lax.all_gather(decode_attn, 'req', axis=0, tiled=True)  28.9 us
    dynamic_slice x36, local copies, waits for them, and re-layouts, take(): lax.dynamic_index_in_dim(a, source, 0, False)  27.4 us
    mul x31, other arithmetic, combine(): second_sum * second_scale[..., None]  21.9 us
    mul x31, other arithmetic, combine(): first_sum * first_scale[..., None] + second_sum * second_scale[..., None]  21.4 us
    all_gather x1, waiting for transfers between devices, merged(): gathered = jax.tree.map(lambda a: lax.all_gather(a, axis), part)  13 us
    add x31, other arithmetic, combine(): first_sum * first_scale[..., None] + second_sum * second_scale[..., None]  12 us
  transfers between devices with their start and end apart: 6, of which 3 were waited for; matrix products, arithmetic and copies ran while one was open for 36% of the time, Pallas kernels for 0%

profile of v1, /device:TPU:6, one launch (start us, length us, event | category | flops | bytes accessed | tf_op | source)
XLA Modules:
  0.0 330.6 jit_solution(3615379111863960665)
XLA Ops:
  8.0 3.9 %copy.83 = bf16[16,128,512]{1,2,0:T(8,128)(2,1)} copy(bf16[16,128,512]{2,1,0:T(8,128)(2,1)} %param.16) | data formatting | bytes 4194304 | tf_op args[5]
  12.0 2.5 broadcast_select_fusion
  15.1 1.3 fusion.28
  17.3 11.6 %all-to-all-start = ((bf16[32,1,16,512]{3,2,1,0:T(8,128)(2,1)}), bf16[32,1,16,512]{3,2,1,0:T(8,128)(2,1)S(1)}, u32[]{:S(2)}, u32[]{:S(2)}) async-start(bf16[32,1,16,512]{3,2,1,0:T(8,128)(2,1)} %stack.2), calls=%async_computation | async-start | bytes 1048576 | tf_op jit(solution)/shard_map/all_to_all | solution.py:16
  28.9 2.6 copy.95
  32.2 44.1 %all-gather = f32[512,2,4]{2,1,0:T(2,128)S(1)} all-gather(f32[16,2,4]{2,1,0:T(2,128)S(1)} %get-tuple-element.249), channel_id=2, replica_groups=mesh['blk'=32,'req'=8] {'blk'}, dimensions={0}, use_global_device_ids=true | all-gather | bytes 16896 | tf_op jit(solution)/shard_map/all_gather | solution.py:24
  76.6 38.3 %all-gather.1 = f32[512,2,4]{2,1,0:T(2,128)S(1)} all-gather(f32[16,2,4]{2,1,0:T(2,128)S(1)} %fusion.26), channel_id=3, replica_groups=mesh['blk'=32,'req'=8] {'blk'}, dimensions={0}, use_global_device_ids=true | all-gather | bytes 16896 | tf_op jit(solution)/shard_map/all_gather | solution.py:24
  115.0 1.1 copy.91
  116.1 1.1 copy.92
  117.5 1.2 gather_fusion
  119.1 1.5 copy.70
  121.4 1.4 reshape.393
  122.8 6.1 %all-to-all-start.2 = ((f32[32,1,128]{2,1,0:T(1,128)}), f32[32,1,128]{2,1,0:T(1,128)S(1)}, u32[]{:S(2)}, u32[]{:S(2)}) async-start(f32[32,1,128]{2,1,0:T(1,128)} %reshape.393), calls=%async_computation.2 | async-start | bytes 32768 | tf_op jit(solution)/shard_map/all_to_all | solution.py:131
  129.8 1.4 reshape.395
  131.1 4.9 %all-to-all-done.2 = f32[32,1,128]{2,1,0:T(1,128)S(1)} async-done(((f32[32,1,128]{2,1,0:T(1,128)}), f32[32,1,128]{2,1,0:T(1,128)S(1)}, u32[]{:S(2)}, u32[]{:S(2)}) %all-to-all-start.2) | async-done | bytes 16416 | tf_op jit(solution)/shard_map/all_to_all | solution.py:131
  136.0 6.7 %all-to-all-start.3 = ((f32[32,1,128]{2,1,0:T(1,128)}), f32[32,1,128]{2,1,0:T(1,128)S(1)}, u32[]{:S(2)}, u32[]{:S(2)}) async-start(f32[32,1,128]{2,1,0:T(1,128)} %reshape.395), calls=%async_computation.3 | async-start | bytes 32768 | tf_op jit(solution)/shard_map/all_to_all | solution.py:132
  143.4 2.6 copy.76
  148.7 1.1 all-to-all-done.3
  149.7 8.8 %all-to-all-start.1 = ((f32[1,1,2,4,512,128]{5,3,2,1,0,4:T(4,128)}), f32[1,1,2,4,512,128]{5,3,2,1,0,4:T(4,128)S(1)}, u32[]{:S(2)}, u32[]{:S(2)}) async-start(f32[1,1,2,4,512,128]{5,3,2,1,0,4:T(4,128)} %copy.76), calls=%async_computation.1 | async-start | bytes 4194304 | tf_op jit(solution)/shard_map/all_to_all | solution.py:133
  160.7 13.0 %all-gather.8.cloned.1.call-done = f32[512,2,4,128]{3,2,1,0:T(4,128)} async-done(((f32[16,2,4,128]{3,2,1,0:T(4,128)}), f32[512,2,4,128]{3,2,1,0:T(4,128)}) %all-gather.8.cloned.1.call-update) | async-done | bytes 2097168 | tf_op jit(solution)/shard_map/all_gather | solution.py:24
  174.6 88.2 %while.19 = (s32[]{:T(128)}, f32[16,2,4,1]{0,2,3,1:T(4,128)S(1)}, f32[16,2,4,1]{0,2,3,1:T(4,128)S(1)}, f32[16,2,4,1,128]{4,3,2,1,0:T(1,128)S(1)}, f32[32,16,2,4,...) while((s32[]{:T(128)}, f32[16,2,4,1]{0,2,3,1:T(4,128)S(1)}, ...), condition=%wide.region_8.9_spmd, body=%wide.region_7.8_spmd.sunk | while | flops 50053 | bytes 337563 | solution.py:29
  176.0 0.9 constant_dynamic-slice_fusion.2
  178.8 0.9 constant_dynamic-slice_fusion.2
  187.3 0.9 constant_dynamic-slice_fusion.2
  190.2 0.9 constant_dynamic-slice_fusion.2
  193.0 0.9 constant_dynamic-slice_fusion.2
  195.9 0.9 constant_dynamic-slice_fusion.2
  201.6 0.9 constant_dynamic-slice_fusion.2
  207.3 0.9 constant_dynamic-slice_fusion.2
  210.1 0.9 constant_dynamic-slice_fusion.2
  263.2 28.9 %all_gather.35 = bf16[128,1024]{1,0:T(8,128)(2,1)S(1)} all-gather(bf16[16,1024]{1,0:T(8,128)(2,1)S(1)} %convert_element_type.51), channel_id=1, replica_groups=mesh['blk'=32,'req'=8] {'req'}, dimensions={0}, use_global_device_ids=true | all-gather | bytes 294912 | tf_op jit(solution)/shard_map/all_gather | solution.py:142
  293.8 29.0 %all_gather.28 = bf16[8,16,1024]{2,1,0:T(8,128)(2,1)S(1)} all-gather(bf16[1,16,1024]{2,1,0:T(8,128)(2,1)S(1)} %convert_element_type.46), channel_id=1, replica_groups=mesh['blk'=32,'req'=8] {'req'}, dimensions={0}, use_global_device_ids=true | all-gather | bytes 294912 | tf_op jit(solution)/shard_map/all_gather | solution.py:141
  (278 shorter events, 94.2 us)
Async XLA Ops:
  7.2 111.9 %all-gather.6.cloned.1.call-start = ((), (), s32[]{:S(2)}) async-start(), calls=%async_computation.4 | async-start | bytes 1081344 | tf_op jit(solution)/shard_map/all_gather | solution.py:123
  7.9 165.8 %all-gather.8.cloned.1.call-start = ((), (), s32[]{:S(2)}) async-start(), calls=%async_computation.5 | async-start | bytes 2162688 | tf_op jit(solution)/shard_map/all_gather | solution.py:24
  8.0 4.0 %copy-start.2 = (bf16[16,1024]{1,0:T(8,128)(2,1)S(1)}, bf16[16,1024]{1,0:T(8,128)(2,1)}, u32[]{:S(2)}) copy-start(bf16[16,1024]{1,0:T(8,128)(2,1)} %param.12) | copy-start | bytes 98308
  8.0 4.0 %copy-start.6 = (s32[16]{0:T(128)S(1)}, s32[16]{0:T(128)}, u32[]{:S(2)}) copy-start(s32[16]{0:T(128)} %param.18) | copy-start | bytes 196
  8.0 4.1 %copy-start.3 = (bf16[16,512]{1,0:T(8,128)(2,1)S(1)}, bf16[16,512]{1,0:T(8,128)(2,1)}, u32[]{:S(2)}) copy-start(bf16[16,512]{1,0:T(8,128)(2,1)} %param.14) | copy-start | bytes 49156
  14.7 1.8 copy-start.4
  17.3 100.2 %all-to-all-start = ((bf16[32,1,16,512]{3,2,1,0:T(8,128)(2,1)}), bf16[32,1,16,512]{3,2,1,0:T(8,128)(2,1)S(1)}, u32[]{:S(2)}, u32[]{:S(2)}) async-start(bf16[32,1,16,512]{3,2,1,0:T(8,128)(2,1)} %stack.2), calls=%async_computation | async-start | bytes 1048576 | tf_op jit(solution)/shard_map/all_to_all | solution.py:16
  31.5 85.7 %copy-start.5 = (s32[136]{0:T(256)S(1)}, s32[136]{0:T(256)}, u32[]{:S(2)}) copy-start(s32[136]{0:T(256)} %param.19) | copy-start | bytes 1636
  31.5 87.1 %copy-start.1 = (bf16[1,128,512]{2,1,0:T(8,128)(2,1)S(1)}, bf16[1,128,512]{2,1,0:T(8,128)(2,1)}, u32[]{:S(2)}) copy-start(bf16[1,128,512]{2,1,0:T(8,128)(2,1)} %param.15) | copy-start | bytes 393220
  118.8 2.4 copy-start
  122.8 13.2 %all-to-all-start.2 = ((f32[32,1,128]{2,1,0:T(1,128)}), f32[32,1,128]{2,1,0:T(1,128)S(1)}, u32[]{:S(2)}, u32[]{:S(2)}) async-start(f32[32,1,128]{2,1,0:T(1,128)} %reshape.393), calls=%async_computation.2 | async-start | bytes 32768 | tf_op jit(solution)/shard_map/all_to_all | solution.py:131
  136.0 13.7 %all-to-all-start.3 = ((f32[32,1,128]{2,1,0:T(1,128)}), f32[32,1,128]{2,1,0:T(1,128)S(1)}, u32[]{:S(2)}, u32[]{:S(2)}) async-start(f32[32,1,128]{2,1,0:T(1,128)} %reshape.395), calls=%async_computation.3 | async-start | bytes 32768 | tf_op jit(solution)/shard_map/all_to_all | solution.py:132
  149.7 143.2 %all-to-all-start.1 = ((f32[1,1,2,4,512,128]{5,3,2,1,0,4:T(4,128)}), f32[1,1,2,4,512,128]{5,3,2,1,0,4:T(4,128)S(1)}, u32[]{:S(2)}, u32[]{:S(2)}) async-start(f32[1,1,2,4,512,128]{5,3,2,1,0,4:T(4,128)} %copy.76), calls=%async_computation.1 | async-start | bytes 4194304 | tf_op jit(solution)/shard_map/all_to_all | solution.py:133
Sparse Core Ops, SparseCore 0:
  10.8 79.4 all-gather.5
  93.0 80.6 all-gather.7
